TPU v7x, 32 devices: a whole 2x2x4 slice. The times are simulated.
32 devices in a mesh: snap: 4 (over z), cell: 8 (over y, x, core).
Axes of the slice: x: 2, y: 2, z: 4, core: 2. Of those that a mesh axis runs over, the one named last changes fastest.
Arguments:
- pressure: float32 [8320, 16384], P('snap', 'cell'), may hold values from -180 to 180
- block_starts: int32 [64], replicated, may hold values from 0 to 8064, as said below
- retained_bins: int32 [64], replicated, may hold values from 0 to 127
Outputs:
- spectral_gram: float32 [64, 2, 64, 64], P('snap')
Inputs may be any that keep to these rules, and one draw needn't show every extreme that they name: `block_starts`: the 64 values are distinct multiples of 128.
All inputs are finite; a program needn't handle non-finite values.
Results may differ from a plain program's by a relative error of at most 0.0003.
Values sent between devices are 32-bit elements; how exact they have to be, the bound alone decides.
A program may use at most 128 MiB of HBM per device.

v0:
```python
import jax
import jax.numpy as jnp
from jax import lax
from jax.sharding import PartitionSpec as P

NFFT = 256


def make_table(retained_bins):
    offsets = jnp.arange(NFFT, dtype=jnp.int32)
    window = 0.5 - 0.5 * jnp.cos(2.0 * jnp.pi * offsets.astype(jnp.float32) / NFFT)
    norm_factor = 1.0 / jnp.sqrt(jnp.sum(window * window))
    phase_steps = retained_bins[:, None] * offsets[None, :] % NFFT
    angles = 2.0 * jnp.pi * phase_steps.astype(jnp.float32) / NFFT
    wave_table = jnp.stack(
        [window * norm_factor * jnp.cos(angles), -window * norm_factor * jnp.sin(angles)], 1
    )
    return wave_table.reshape(2 * retained_bins.shape[0], NFFT)


def on_device(pressure, block_starts, retained_bins):
    snap_count = lax.axis_size("snap")
    row_count, width_local = pressure.shape
    pieces = width_local // snap_count
    shaped = pressure.reshape(row_count, snap_count, pieces)
    wave_table = make_table(retained_bins)
    half_len = NFFT // 2
    front_table = wave_table[:, :half_len]
    back_table = wave_table[:, half_len:]
    segment_ids = block_starts // half_len
    series = lax.all_to_all(shaped, "snap", split_axis=1, concat_axis=0, tiled=True)[:, 0, :]
    segments = series.reshape(series.shape[0] // half_len, half_len, series.shape[1])
    front_part = jnp.einsum("rt,stc->rsc", front_table, segments, precision=lax.Precision.HIGHEST)
    second = jnp.einsum("rt,stc->rsc", back_table, segments, precision=lax.Precision.HIGHEST)
    spectra = jnp.take(front_part, segment_ids, axis=1) + jnp.take(second, segment_ids + 1, axis=1)
    kept_count = retained_bins.shape[0]
    blocks = block_starts.shape[0]
    stacked = spectra.reshape(kept_count, 2 * blocks, spectra.shape[2])
    products = jnp.einsum("kbc,kdc->kbd", stacked, stacked, precision=lax.Precision.HIGHEST)
    real_part = products[:, :blocks, :blocks] + products[:, blocks:, blocks:]
    imag_part = products[:, :blocks, blocks:] - products[:, blocks:, :blocks]
    local_gram = jnp.stack([real_part, imag_part], 1)
    cell_total = width_local * lax.axis_size("cell")
    partial_gram = lax.psum_scatter(local_gram, "snap", scatter_dimension=0, tiled=True)
    own_block = lax.psum(partial_gram, "cell")
    return own_block / cell_total


def solution(mesh):
    placed = (P("snap", "cell"), P(), P())
    return jax.shard_map(
        on_device,
        mesh=mesh,
        in_specs=placed,
        out_specs=P("snap", None, None, None),
        check_vma=False,
    )
```

profile of v0, /device:TPU:0, one launch (start us, length us, event | category | flops | bytes accessed | tf_op | source)
XLA Modules:
  0.0 645.2 jit_solution(13839969058328728660)
XLA Ops:
  6.5 11.7 %copy.23 = f32[260,4,8,512]{3,2,0,1:T(8,128)} copy(f32[260,4,8,512]{3,2,1,0:T(8,128)} %bitcast.34) | data formatting | bytes 34078720 | tf_op jit(solution)/shard_map/reshape | solution.py:25
  18.3 0.0 copy-start
  18.3 0.0 copy-start.1
  18.3 7.1 %all-to-all-start = ((f32[2080,4,512]{2,0,1:T(8,128)}), f32[2080,4,512]{2,0,1:T(8,128)}, u32[]{:S(2)}, u32[]{:S(2)}) async-start(f32[2080,4,512]{2,0,1:T(8,128)} %bitcast.33), calls=%async_computation | async-start | bytes 34078720 | tf_op jit(solution)/shard_map/all_to_all | solution.py:31
  25.4 0.0 reduce-scatter.4.cloned.1.call-start
  25.5 0.6 multiply_reduce_fusion
  26.9 0.0 copy-done
  26.9 0.3 cosine_multiply_fusion
  27.2 0.1 copy.15
  27.4 0.1 reshape.161
  27.5 0.0 copy-done.1
  27.5 368.1 %all-to-all-done = f32[2080,4,512]{2,0,1:T(8,128)} async-done(((f32[2080,4,512]{2,0,1:T(8,128)}), f32[2080,4,512]{2,0,1:T(8,128)}, u32[]{:S(2)}, u32[]{:S(2)}) %all-to-all-start) | async-done | bytes 17039392 | tf_op jit(solution)/shard_map/all_to_all | solution.py:31
  395.7 21.9 %fusion.5 = f32[128,65,512]{2,0,1:T(8,128)} fusion(f32[65,128,512]{2,1,0:T(8,128)} %bitcast.3, f32[128,256]{1,0:T(8,128)S(1)} %reshape.161), kind=kOutput, calls=%fused_computation.18 | convolution fusion | flops 6543114240 | bytes 34144256 | tf_op jit(solution)/shard_map/rt,stc->rsc/dot_general | solution.py:34
  417.6 22.0 %fusion.6 = f32[128,65,512]{2,0,1:T(8,128)} fusion(f32[65,128,512]{2,1,0:T(8,128)} %bitcast.3, f32[128,256]{1,0:T(8,128)S(1)} %reshape.161), kind=kOutput, calls=%fused_computation.20 | convolution fusion | flops 6543114240 | bytes 34144256 | tf_op jit(solution)/shard_map/rt,stc->rsc/dot_general | solution.py:33
  439.6 14.7 %gather_fusion.1 = f32[64,128,512]{2,1,0:T(8,128)} fusion(f32[128,65,512]{2,0,1:T(8,128)} %fusion.5, s32[1024]{0:T(1024)S(1)} %pad_clamp_fusion), kind=kCustom, calls=%fused_computation.1.clone | custom fusion | bytes 33554688 | tf_op jit(solution)/shard_map/jit(_take)/gather | solution.py:35
  454.3 14.7 %gather_fusion = f32[64,128,512]{2,1,0:T(8,128)} fusion(f32[128,65,512]{2,0,1:T(8,128)} %fusion.6, s32[1024]{0:T(1024)S(1)} %pad_clamp_fusion.1), kind=kCustom, calls=%fused_computation.clone | custom fusion | bytes 33554688 | tf_op jit(solution)/shard_map/jit(_take)/gather | solution.py:35
  469.0 12.0 %bitcast_add_fusion = f32[128,64,512]{2,0,1:T(8,128)S(1)} fusion(f32[64,128,512]{2,1,0:T(8,128)} %gather_fusion.1, f32[64,128,512]{2,1,0:T(8,128)} %gather_fusion, pred[64]{0:T(512)(128)(4,1)S(1)} %get-tuple-element.8, pred[64]{0:T(512)(128)(4,1)S(1)} %get-tuple-element.6), kind=kLoop, calls=%fused_computation.3 | loop fusion | flops 12582912 | bytes 50331776 | tf_op jit(solution)/shard_map/add | solution.py:35
  481.0 19.5 %copy.17 = f32[128,64,512]{2,1,0:T(8,128)} copy(f32[128,64,512]{2,0,1:T(8,128)S(1)} %bitcast_add_fusion) | data formatting | bytes 33554432 | tf_op jit(solution)/shard_map/add | solution.py:35
  500.5 21.4 %fusion.10 = f32[64,128,128]{2,1,0:T(8,128)} fusion(f32[64,128,512]{2,1,0:T(8,128)} %bitcast.32), kind=kOutput, calls=%fused_computation.40 | convolution fusion | flops 6442450944 | bytes 20971520 | tf_op jit(solution)/shard_map/kbc,kdc->kbd/dot_general | solution.py:39
  521.9 4.6 fusion.1
  526.6 0.4 pad_maximum_fusion
  527.0 2.3 copy.19
  529.3 4.8 reshape.188
  534.0 0.0 reduce-scatter.4.cloned.1.call-update
  534.0 0.0 all-reduce.2.cloned.1.call-start
  534.1 42.8 %reduce-scatter.4.cloned.1.call-done = f32[16,8192]{1,0:T(8,128)} async-done(((f32[64,8192]{1,0:T(8,128)}), f32[16,8192]{1,0:T(8,128)}) %reduce-scatter.4.cloned.1.call-update) | async-done | bytes 524304
  576.9 1.5 reshape.189
  578.4 1.0 copy.20
  579.4 0.0 all-reduce.2.cloned.1.call-update
  579.4 56.5 %all-reduce.2.cloned.1.call-done = f32[16,2,64,64]{3,2,0,1:T(8,128)} async-done(((f32[16,2,64,64]{3,2,0,1:T(8,128)}), f32[16,2,64,64]{3,2,0,1:T(8,128)}) %all-reduce.2.cloned.1.call-update) | async-done | bytes 524304 | tf_op jit(solution)/shard_map/psum | solution.py:45
  636.0 1.3 broadcast_multiply_fusion
  637.3 1.1 copy.18
  (7 shorter events, 0.1 us)
Async XLA Ops:
  18.3 8.6 %copy-start = (s32[64]{0:T(128)S(1)}, s32[64]{0:T(128)}, u32[]{:S(2)}) copy-start(s32[64]{0:T(128)} %param.7) | copy-start | bytes 772
  18.3 9.2 %copy-start.1 = (s32[64]{0:T(128)S(1)}, s32[64]{0:T(128)}, u32[]{:S(2)}) copy-start(s32[64]{0:T(128)} %param.6) | copy-start | bytes 772
  18.3 377.4 %all-to-all-start = ((f32[2080,4,512]{2,0,1:T(8,128)}), f32[2080,4,512]{2,0,1:T(8,128)}, u32[]{:S(2)}, u32[]{:S(2)}) async-start(f32[2080,4,512]{2,0,1:T(8,128)} %bitcast.33), calls=%async_computation | async-start | bytes 34078720 | tf_op jit(solution)/shard_map/all_to_all | solution.py:31
  25.4 551.5 %reduce-scatter.4.cloned.1.call-start = ((), (), s32[]{:S(2)}) async-start(), calls=%async_computation.3 | async-start | bytes 2621440
  534.0 101.9 %all-reduce.2.cloned.1.call-start = ((), (), s32[]{:S(2)}) async-start(), calls=%async_computation.2 | async-start | bytes 2097152 | tf_op jit(solution)/shard_map/psum | solution.py:45
Sparse Core Ops, SparseCore 0:
  534.2 42.6 reduce-scatter.3
  580.1 55.8 all-reduce.1
where the time goes:
time: 646 us; the launch traced here: 645 us
  waiting for transfers between devices  468 us (72%)
  local copies, waits for them, and re-layouts  71.5 us (11%)
  matrix products  65.3 us (10%)
  other arithmetic  19.5 us (3%)
  between operations  14.2 us (2%)
  starting transfers between devices  7.22 us (1%)
    all_to_all x1, waiting for transfers between devices, on_device(): lax.all_to_all(shaped, 'snap', split_axis=1, concat_axis=0, tiled=True)  368 us
    psum x1, waiting for transfers between devices, on_device(): own_block = lax.psum(partial_gram, 'cell')  56.5 us
    unnamed x3, waiting for transfers between devices  42.8 us
    dot_general x1, matrix products, on_device(): jnp.einsum('rt,stc->rsc', front_table, segments, precision=lax.Precision....  22 us
    dot_general x1, matrix products, on_device(): jnp.einsum('rt,stc->rsc', back_table, segments, precision=lax.Precision.H...  21.9 us
    dot_general x1, matrix products, on_device(): jnp.einsum('kbc,kdc->kbd', stacked, stacked, precision=lax.Precision.HIGH...  21.4 us
    add x1, local copies, waits for them, and re-layouts, on_device(): jnp.take(front_part, segment_ids, axis=1)  19.5 us
    gather x1, local copies, waits for them, and re-layouts, on_device(): jnp.take(second, segment_ids + 1, axis=1)  14.7 us
  transfers between devices with their start and end apart: 3, of which 3 were waited for; matrix products, arithmetic and copies ran while one was open for 0% of the time, Pallas kernels for 0%

commit v1 on v0

v1 whole, which is shorter than its diff:
```python
import jax
import jax.numpy as jnp
from jax import lax
from jax.sharding import PartitionSpec as P

NFFT = 256
LANES = 128
MAX_CHUNKS = 4


def make_table(retained_bins):
    offsets = jnp.arange(NFFT, dtype=jnp.int32)
    window = 0.5 - 0.5 * jnp.cos(2.0 * jnp.pi * offsets.astype(jnp.float32) / NFFT)
    norm_factor = 1.0 / jnp.sqrt(jnp.sum(window * window))
    phase_steps = retained_bins[:, None] * offsets[None, :] % NFFT
    angles = 2.0 * jnp.pi * phase_steps.astype(jnp.float32) / NFFT
    wave_table = jnp.stack(
        [window * norm_factor * jnp.cos(angles), -window * norm_factor * jnp.sin(angles)], 1
    )
    return wave_table.reshape(2 * retained_bins.shape[0], NFFT)


def chunk_products(series, wave_table, kept_count, blocks):
    half_len = NFFT // 2
    segments = series.reshape(series.shape[0] // half_len, half_len, series.shape[1])
    front = jnp.einsum("rt,stc->rsc", wave_table[:, :half_len], segments[:-1], precision=lax.Precision.HIGHEST)
    back = jnp.einsum("rt,stc->rsc", wave_table[:, half_len:], segments[1:], precision=lax.Precision.HIGHEST)
    stacked = (front + back).reshape(kept_count, 2 * blocks, series.shape[1])
    return jnp.einsum("kbc,kdc->kbd", stacked, stacked, precision=lax.Precision.HIGHEST)


def on_device(pressure, block_starts, retained_bins):
    snap_count = lax.axis_size("snap")
    row_count, width_local = pressure.shape
    pieces = width_local // snap_count
    chunks = max(n for n in range(1, MAX_CHUNKS + 1) if pieces % (n * LANES) == 0)
    wide = pieces // chunks
    wave_table = make_table(retained_bins)
    kept_count = retained_bins.shape[0]
    blocks = block_starts.shape[0]
    received = []
    for i in range(chunks):
        columns = pressure[:, i * snap_count * wide:(i + 1) * snap_count * wide]
        shaped = columns.reshape(row_count, snap_count, wide)
        received.append(lax.all_to_all(shaped, "snap", split_axis=1, concat_axis=0, tiled=True)[:, 0, :])
    products = chunk_products(received[0], wave_table, kept_count, blocks)
    for series in received[1:]:
        products = products + chunk_products(series, wave_table, kept_count, blocks)
    real_part = products[:, :blocks, :blocks] + products[:, blocks:, blocks:]
    imag_part = products[:, :blocks, blocks:] - products[:, blocks:, :blocks]
    local_gram = jnp.stack([real_part, imag_part], 1)
    cell_total = width_local * lax.axis_size("cell")
    partial_gram = lax.psum_scatter(local_gram, "snap", scatter_dimension=0, tiled=True)
    own_block = lax.psum(partial_gram, "cell") / cell_total
    order = (block_starts[:, None] // (NFFT // 2) == jnp.arange(blocks)[None, :]).astype(jnp.float32)
    turned = jnp.einsum("kpij,dj->kpid", own_block, order, precision=lax.Precision.HIGHEST)
    return jnp.einsum("bi,kpid->kpbd", order, turned, precision=lax.Precision.HIGHEST)


def solution(mesh):
    placed = (P("snap", "cell"), P(), P())
    return jax.shard_map(
        on_device,
        mesh=mesh,
        in_specs=placed,
        out_specs=P("snap", None, None, None),
        check_vma=False,
    )
```

time: 646 us -> 570 us (0.88)
  waiting for transfers between devices: 468 us -> 389 us
  matrix products: 65.3 us -> 89.9 us
  local copies, waits for them, and re-layouts: 71.5 us -> 48.6 us
  other arithmetic: 19.5 us -> 2.63 us
  starting transfers between devices: 7.22 us -> 21.4 us
    all_to_all x1 -> x4, waiting for transfers between devices: 368 us -> 290 us  [on_device(): lax.all_to_all(shaped, 'snap', split_axis=1, concat_axis=0, tiled=True)]
    gather x2 -> x0, local copies, waits for them, and re-layouts: 29.4 us -> none  [the longest x1 14.7 us: on_device(): jnp.take(second, segment_ids + 1, axis=1)]
    dot_general x3 -> x14, matrix products: 65.3 us -> 89.9 us  [the longest x4 42.4 us: chunk_products(): jnp.einsum('kbc,kdc->kbd', stacked, stacked, precision=lax.Precision.HIGH...]
    all_to_all x1 -> x4, starting transfers between devices: 7.14 us -> 21.1 us  [on_device(): lax.all_to_all(shaped, 'snap', split_axis=1, concat_axis=0, tiled=True)]
    add x1 -> x0, other arithmetic: 12 us -> none  [on_device(): jnp.take(front_part, segment_ids, axis=1)]
    add x1 -> x4, local copies, waits for them, and re-layouts: 19.5 us -> 9.72 us  [chunk_products(): stacked = (front + back).reshape(kept_count, 2 * blocks, series.shape[1])]
    unnamed x8 -> x11, local copies, waits for them, and re-layouts: 9.52 us -> 19.2 us
    reshape x1 -> x4, local copies, waits for them, and re-layouts: 11.7 us -> 15.7 us  [on_device(): shaped = columns.reshape(row_count, snap_count, wide)]
  transfers between devices with their start and end apart: 3 -> 6, of which waited for: 3 -> 6; matrix products, arithmetic and copies ran while one was open for 0% -> 15% of each run, Pallas kernels for 0% -> 0%
where the time goes in v1:
time: 570 us; the launch traced here: 566 us
  waiting for transfers between devices  389 us (68%)
  matrix products  89.9 us (16%)
  local copies, waits for them, and re-layouts  48.6 us (9%)
  starting transfers between devices  21.4 us (4%)
  between operations  14.5 us (3%)
    all_to_all x4, waiting for transfers between devices, on_device(): lax.all_to_all(shaped, 'snap', split_axis=1, concat_axis=0, tiled=True)  290 us
    psum x1, waiting for transfers between devices, on_device(): own_block = lax.psum(partial_gram, 'cell') / cell_total  56.6 us
    unnamed x3, waiting for transfers between devices  43 us
    dot_general x4, matrix products, chunk_products(): jnp.einsum('kbc,kdc->kbd', stacked, stacked, precision=lax.Precision.HIGH...  42.4 us
    dot_general x4, matrix products, chunk_products(): jnp.einsum('rt,stc->rsc', wave_table[:, :half_len], segments[:-1], precis...  22.4 us
    dot_general x4, matrix products, chunk_products(): jnp.einsum('rt,stc->rsc', wave_table[:, half_len:], segments[1:], precisi...  21.6 us
    all_to_all x4, starting transfers between devices, on_device(): lax.all_to_all(shaped, 'snap', split_axis=1, concat_axis=0, tiled=True)  21.1 us
    unnamed x11, local copies, waits for them, and re-layouts  19.2 us
  transfers between devices with their start and end apart: 6, of which 6 were waited for; matrix products, arithmetic and copies ran while one was open for 15% of the time, Pallas kernels for 0%

profile of v1, /device:TPU:0, one launch (start us, length us, event | category | flops | bytes accessed | tf_op | source)
XLA Modules:
  0.0 566.3 jit_solution(12413010602740145262)
XLA Ops:
  6.5 11.2 %slice_bitcast_fusion = (f32[260,4,8,128]{3,2,1,0:T(8,128)}, f32[260,4,8,128]{3,2,1,0:T(8,128)}, f32[260,4,8,128]{3,2,1,0:T(8,128)}, f32[260,4,8,128]{3,2,1,0:T(8,128)S(1)}) fusion(f32[2080,2048]{1,0:T(8,128)} %param.3), kind=kLoop, calls=%fused_computation.4 | loop fusion | bytes 34078720
  20.0 6.3 %all-to-all-start.2 = ((f32[2080,4,128]{2,0,1:T(8,128)}), f32[2080,4,128]{2,0,1:T(8,128)}, u32[]{:S(2)}, u32[]{:S(2)}) async-start(f32[2080,4,128]{2,0,1:T(8,128)} %bitcast.88), calls=%async_computation.2 | async-start | bytes 8519680 | tf_op jit(solution)/shard_map/all_to_all | solution.py:45
  26.4 4.5 copy.67
  30.8 90.4 %all-to-all-done.2 = f32[2080,4,128]{2,0,1:T(8,128)} async-done(((f32[2080,4,128]{2,0,1:T(8,128)}), f32[2080,4,128]{2,0,1:T(8,128)}, u32[]{:S(2)}, u32[]{:S(2)}) %all-to-all-start.2) | async-done | bytes 4259872 | tf_op jit(solution)/shard_map/all_to_all | solution.py:45
  121.2 4.9 all-to-all-start
  126.2 4.5 copy.66
  130.7 89.5 %all-to-all-done = f32[2080,4,128]{2,0,1:T(8,128)} async-done(((f32[2080,4,128]{2,0,1:T(8,128)}), f32[2080,4,128]{2,0,1:T(8,128)}, u32[]{:S(2)}, u32[]{:S(2)}) %all-to-all-start) | async-done | bytes 4259872 | tf_op jit(solution)/shard_map/all_to_all | solution.py:45
  220.2 4.9 all-to-all-start.1
  225.1 4.4 copy.64
  229.5 89.7 %all-to-all-done.1 = f32[2080,4,128]{2,0,1:T(8,128)} async-done(((f32[2080,4,128]{2,0,1:T(8,128)}), f32[2080,4,128]{2,0,1:T(8,128)}, u32[]{:S(2)}, u32[]{:S(2)}) %all-to-all-start.1) | async-done | bytes 4259872 | tf_op jit(solution)/shard_map/all_to_all | solution.py:45
  319.2 5.0 all-to-all-start.3
  326.4 5.4 fusion.4
  331.8 5.4 fusion.22
  337.2 2.4 copy.46
  339.6 5.4 fusion.12
  345.0 5.9 %fusion.16 = f32[128,64,128]{2,0,1:T(8,128)S(1)} fusion(f32[128,64,128]{2,0,1:T(8,128)S(1)} %fusion.12, f32[65,128,128]{2,1,0:T(8,128)} %bitcast.3, f32[128,256]{1,0:T(8,128)S(1)} %reshape.196), kind=kOutput, calls=%fused_computation.26 | convolution fusion | flops 1611661312 | bytes 12648448 | tf_op jit(solution)/shard_map/rt,stc->rsc/dot_general | solution.py:26
  350.9 2.4 copy.42
  353.4 5.4 fusion.8
  358.8 5.7 %fusion.19 = f32[128,64,128]{2,0,1:T(8,128)S(1)} fusion(f32[128,64,128]{2,0,1:T(8,128)S(1)} %fusion.8, f32[65,128,128]{2,1,0:T(8,128)} %bitcast.10, f32[128,256]{1,0:T(8,128)S(1)} %reshape.196), kind=kOutput, calls=%fused_computation.27 | convolution fusion | flops 1611661312 | bytes 12648448 | tf_op jit(solution)/shard_map/rt,stc->rsc/dot_general | solution.py:26
  366.9 10.3 %fusion.47 = f32[64,128,128]{2,1,0:T(8,128)} fusion(f32[64,128,128]{2,1,0:T(8,128)S(1)} %bitcast.82), kind=kOutput, calls=%fused_computation.67 | convolution fusion | flops 1610612736 | bytes 8388608 | tf_op jit(solution)/shard_map/kbc,kdc->kbd/dot_general | solution.py:29
  377.2 10.7 %fusion.45 = f32[64,128,128]{2,1,0:T(8,128)} fusion(f32[64,128,128]{2,1,0:T(8,128)S(1)} %bitcast.83), kind=kOutput, calls=%fused_computation.65 | convolution fusion | flops 1610612736 | bytes 8388608 | tf_op jit(solution)/shard_map/kbc,kdc->kbd/dot_general | solution.py:29
  388.0 10.3 %fusion.46 = f32[64,128,128]{2,1,0:T(8,128)} fusion(f32[64,128,128]{2,1,0:T(8,128)S(1)} %bitcast.84), kind=kOutput, calls=%fused_computation.66 | convolution fusion | flops 1610612736 | bytes 8388608 | tf_op jit(solution)/shard_map/kbc,kdc->kbd/dot_general | solution.py:29
  398.2 20.1 %all-to-all-done.3 = f32[2080,4,128]{2,0,1:T(8,128)} async-done(((f32[2080,4,128]{2,0,1:T(8,128)}), f32[2080,4,128]{2,0,1:T(8,128)}, u32[]{:S(2)}, u32[]{:S(2)}) %all-to-all-start.3) | async-done | bytes 4259872 | tf_op jit(solution)/shard_map/all_to_all | solution.py:45
  418.4 5.4 fusion
  423.7 5.4 fusion.25
  429.2 2.4 copy.48
  432.6 11.1 %add_add_fusion = f32[64,128,128]{2,1,0:T(8,128)S(1)} fusion(f32[64,128,128]{2,1,0:T(8,128)S(1)} %copy-done, f32[64,128,128]{2,1,0:T(8,128)S(1)} %copy-done.1, f32[64,128,128]{2,1,0:T(8,128)} %fusion.46, f32[64,128,128]{2,1,0:T(8,128)S(1)} %bitcast.81), kind=kOutput, calls=%fused_computation.25 | convolution fusion | flops 1613758464 | bytes 20971520 | tf_op jit(solution)/shard_map/kbc,kdc->kbd/dot_general | solution.py:29
  447.6 4.8 reshape.208
  452.4 43.0 %reduce-scatter.4.cloned.1.call-done = f32[16,8192]{1,0:T(8,128)} async-done(((f32[64,8192]{1,0:T(8,128)}), f32[16,8192]{1,0:T(8,128)}) %reduce-scatter.4.cloned.1.call-update) | async-done | bytes 524304
  495.4 2.4 reshape.209
  497.8 56.6 %all-reduce.2.cloned.1.call-done = f32[16,2,64,64]{3,2,1,0:T(8,128)} async-done(((f32[16,2,64,64]{3,2,1,0:T(8,128)}), f32[16,2,64,64]{3,2,1,0:T(8,128)}) %all-reduce.2.cloned.1.call-update) | async-done | bytes 524304 | tf_op jit(solution)/shard_map/psum | solution.py:54
  554.4 2.9 fusion.30
  (26 shorter events, 13.1 us)
Async XLA Ops:
  20.0 101.2 %all-to-all-start.2 = ((f32[2080,4,128]{2,0,1:T(8,128)}), f32[2080,4,128]{2,0,1:T(8,128)}, u32[]{:S(2)}, u32[]{:S(2)}) async-start(f32[2080,4,128]{2,0,1:T(8,128)} %bitcast.88), calls=%async_computation.2 | async-start | bytes 8519680 | tf_op jit(solution)/shard_map/all_to_all | solution.py:45
  121.2 99.0 %all-to-all-start = ((f32[2080,4,128]{2,0,1:T(8,128)}), f32[2080,4,128]{2,0,1:T(8,128)}, u32[]{:S(2)}, u32[]{:S(2)}) async-start(f32[2080,4,128]{2,0,1:T(8,128)} %bitcast.87), calls=%async_computation | async-start | bytes 8519680 | tf_op jit(solution)/shard_map/all_to_all | solution.py:45
  220.2 99.0 %all-to-all-start.1 = ((f32[2080,4,128]{2,0,1:T(8,128)}), f32[2080,4,128]{2,0,1:T(8,128)}, u32[]{:S(2)}, u32[]{:S(2)}) async-start(f32[2080,4,128]{2,0,1:T(8,128)} %bitcast.86), calls=%async_computation.1 | async-start | bytes 8519680 | tf_op jit(solution)/shard_map/all_to_all | solution.py:45
  319.2 6.6 %copy-start.2 = (s32[64]{0:T(128)S(1)}, s32[64]{0:T(128)}, u32[]{:S(2)}) copy-start(s32[64]{0:T(128)} %param.5) | copy-start | bytes 772
  319.2 99.2 %all-to-all-start.3 = ((f32[2080,4,128]{2,0,1:T(8,128)}), f32[2080,4,128]{2,0,1:T(8,128)}, u32[]{:S(2)}, u32[]{:S(2)}) async-start(f32[2080,4,128]{2,0,1:T(8,128)} %bitcast.85), calls=%async_computation.3 | async-start | bytes 8519680 | tf_op jit(solution)/shard_map/all_to_all | solution.py:45
  324.2 171.2 %reduce-scatter.4.cloned.1.call-start = ((), (), s32[]{:S(2)}) async-start(), calls=%async_computation.6 | async-start | bytes 2621440
  429.1 2.5 copy-start
  429.1 3.5 copy-start.1
  447.6 50.3 %copy-start.3 = (s32[64]{0:T(128)S(1)}, s32[64]{0:T(128)}, u32[]{:S(2)}) copy-start(s32[64]{0:T(128)} %param.4) | copy-start | bytes 772
  452.4 102.1 %all-reduce.2.cloned.1.call-start = ((), (), s32[]{:S(2)}) async-start(), calls=%async_computation.5 | async-start | bytes 2097152 | tf_op jit(solution)/shard_map/psum | solution.py:54
Sparse Core Ops, SparseCore 0:
  452.5 42.8 reduce-scatter.3
  498.5 55.8 all-reduce.1

commit v2 on v1

--- a/solution.py
+++ b/solution.py
@@ -1,11 +1,16 @@
+import functools
+
 import jax
 import jax.numpy as jnp
 from jax import lax
+from jax.experimental import pallas as pl
+from jax.experimental.pallas import tpu as pltpu
 from jax.sharding import PartitionSpec as P
 
 NFFT = 256
 LANES = 128
 MAX_CHUNKS = 4
+MESH = pl.DeviceIdType.MESH
 
 
 def make_table(retained_bins):
@@ -29,6 +34,108 @@
     return jnp.einsum("kbc,kdc->kbd", stacked, stacked, precision=lax.Precision.HIGHEST)
 
 
+def reduce_kernel(snap_count, cell_count, scale, gram_ref, out_ref, cell_slots, own_cells, snap_slots, own_part, gathered,
+                  cell_send, cell_recv, snap_send, snap_recv, gather_send, gather_recv):
+    my_snap, my_cell = lax.axis_index("snap"), lax.axis_index("cell")
+
+    def cell_peer(step):
+        return lax.rem(my_cell + step, cell_count)
+
+    def snap_peer(step):
+        return lax.rem(my_snap + step, snap_count)
+
+    barrier = pltpu.get_barrier_semaphore()
+    for step in range(1, cell_count):
+        pl.semaphore_signal(barrier, inc=1, device_id=(my_snap, cell_peer(step)), device_id_type=MESH)
+    for step in range(1, snap_count):
+        pl.semaphore_signal(barrier, inc=1, device_id=(snap_peer(step), my_cell), device_id_type=MESH)
+    pl.semaphore_wait(barrier, cell_count + snap_count - 2)
+
+    scatters = [
+        pltpu.make_async_remote_copy(
+            src_ref=gram_ref.at[cell_peer(step)],
+            dst_ref=cell_slots.at[step - 1],
+            send_sem=cell_send.at[step - 1],
+            recv_sem=cell_recv.at[step - 1],
+            device_id=(my_snap, cell_peer(step)),
+            device_id_type=MESH,
+        )
+        for step in range(1, cell_count)
+    ]
+    for copy in scatters:
+        copy.start()
+    total = gram_ref[my_cell]
+    for step in range(1, cell_count):
+        scatters[step - 1].wait_recv()
+        total = total + cell_slots[step - 1]
+    own_cells[...] = total
+
+    exchanges = [
+        pltpu.make_async_remote_copy(
+            src_ref=own_cells.at[snap_peer(step)],
+            dst_ref=snap_slots.at[step - 1],
+            send_sem=snap_send.at[step - 1],
+            recv_sem=snap_recv.at[step - 1],
+            device_id=(snap_peer(step), my_cell),
+            device_id_type=MESH,
+        )
+        for step in range(1, snap_count)
+    ]
+    for copy in exchanges:
+        copy.start()
+    part = own_cells[my_snap]
+    for step in range(1, snap_count):
+        exchanges[step - 1].wait_recv()
+        part = part + snap_slots[step - 1]
+    own_part[...] = part * scale
+
+    gathers = [
+        pltpu.make_async_remote_copy(
+            src_ref=own_part,
+            dst_ref=gathered.at[my_cell],
+            send_sem=gather_send.at[step - 1],
+            recv_sem=gather_recv.at[step - 1],
+            device_id=(my_snap, cell_peer(step)),
+            device_id_type=MESH,
+        )
+        for step in range(1, cell_count)
+    ]
+    for copy in gathers:
+        copy.start()
+    out_ref[my_cell] = own_part[...]
+    for step in range(1, cell_count):
+        gathers[step - 1].wait_recv()
+        source = lax.rem(my_cell + cell_count - step, cell_count)
+        out_ref[source] = gathered[source]
+    for copy in scatters + exchanges + gathers:
+        copy.wait_send()
+
+
+def reduce_grams(packed, scale):
+    cell_count, snap_count, rows, lanes = packed.shape
+    whole_vmem = pl.BlockSpec(memory_space=pltpu.VMEM)
+    return pl.pallas_call(
+        functools.partial(reduce_kernel, snap_count, cell_count, scale),
+        out_shape=jax.ShapeDtypeStruct((cell_count, rows, lanes), jnp.float32),
+        in_specs=[whole_vmem],
+        out_specs=whole_vmem,
+        scratch_shapes=[
+            pltpu.VMEM((cell_count - 1, snap_count, rows, lanes), jnp.float32),
+            pltpu.VMEM((snap_count, rows, lanes), jnp.float32),
+            pltpu.VMEM((snap_count - 1, rows, lanes), jnp.float32),
+            pltpu.VMEM((rows, lanes), jnp.float32),
+            pltpu.VMEM((cell_count, rows, lanes), jnp.float32),
+            pltpu.SemaphoreType.DMA((cell_count - 1,)),
+            pltpu.SemaphoreType.DMA((cell_count - 1,)),
+            pltpu.SemaphoreType.DMA((snap_count - 1,)),
+            pltpu.SemaphoreType.DMA((snap_count - 1,)),
+            pltpu.SemaphoreType.DMA((cell_count - 1,)),
+            pltpu.SemaphoreType.DMA((cell_count - 1,)),
+        ],
+        compiler_params=pltpu.CompilerParams(collective_id=0, has_side_effects=True),
+    )(packed)
+
+
 def on_device(pressure, block_starts, retained_bins):
     snap_count = lax.axis_size("snap")
     row_count, width_local = pressure.shape
@@ -48,10 +155,20 @@
         products = products + chunk_products(series, wave_table, kept_count, blocks)
     real_part = products[:, :blocks, :blocks] + products[:, blocks:, blocks:]
     imag_part = products[:, :blocks, blocks:] - products[:, blocks:, :blocks]
-    local_gram = jnp.stack([real_part, imag_part], 1)
-    cell_total = width_local * lax.axis_size("cell")
-    partial_gram = lax.psum_scatter(local_gram, "snap", scatter_dimension=0, tiled=True)
-    own_block = lax.psum(partial_gram, "cell") / cell_total
+    lower = jnp.arange(blocks)[:, None] >= jnp.arange(blocks)[None, :]
+    halves = jnp.where(lower, real_part, imag_part)
+    cell_count = lax.axis_size("cell")
+    pairs = kept_count // snap_count // 2
+    rows = pairs * blocks // cell_count
+    split = halves.reshape(snap_count, 2, pairs, blocks, blocks).transpose(0, 2, 3, 1, 4)
+    packed = split.reshape(snap_count, cell_count, rows, 2 * blocks).transpose(1, 0, 2, 3)
+    reduced = reduce_grams(packed, 1.0 / (width_local * cell_count))
+    joined = reduced.reshape(pairs, blocks, 2, blocks).transpose(2, 0, 1, 3).reshape(2 * pairs, blocks, blocks)
+    mirrored = joined.transpose(0, 2, 1)
+    diagonal = jnp.eye(blocks, dtype=bool)
+    own_real = jnp.where(lower, joined, mirrored)
+    own_imag = jnp.where(diagonal, 0.0, jnp.where(lower, -mirrored, joined))
+    own_block = jnp.stack([own_real, own_imag], 1)
     order = (block_starts[:, None] // (NFFT // 2) == jnp.arange(blocks)[None, :]).astype(jnp.float32)
     turned = jnp.einsum("kpij,dj->kpid", own_block, order, precision=lax.Precision.HIGHEST)
     return jnp.einsum("bi,kpid->kpbd", order, turned, precision=lax.Precision.HIGHEST)

time: 570 us -> 476 us (0.84)
  waiting for transfers between devices: 389 us -> 290 us
  Pallas kernels: 0 us -> 24.8 us
  between operations: 14.5 us -> 1.19 us
    psum x1 -> x0, waiting for transfers between devices: 56.6 us -> none  [on_device(): own_block = lax.psum(partial_gram, 'cell') / cell_total]
    unnamed x3 -> x0, waiting for transfers between devices: 43 us -> none
    pallas_call x0 -> x1, Pallas kernels: none -> 24.8 us  [reduce_grams(): pl.pallas_call(functools.partial(reduce_kernel, snap_count, cell_count, s...]
    unnamed x11 -> x9, local copies, waits for them, and re-layouts: 19.2 us -> 12.2 us
  transfers between devices with their start and end apart: 6 -> 4, of which waited for: 6 -> 4; matrix products, arithmetic and copies ran while one was open for 15% -> 18% of each run, Pallas kernels for 0% -> 0%
where the time goes in v2:
time: 476 us; the launch traced here: 473 us
  waiting for transfers between devices  290 us (61%)
  matrix products  88.6 us (19%)
  local copies, waits for them, and re-layouts  44.5 us (9%)
  Pallas kernels  24.8 us (5%)
  starting transfers between devices  21.3 us (4%)
    all_to_all x4, waiting for transfers between devices, on_device(): lax.all_to_all(shaped, 'snap', split_axis=1, concat_axis=0, tiled=True)  290 us
    dot_general x4, matrix products, chunk_products(): jnp.einsum('kbc,kdc->kbd', stacked, stacked, precision=lax.Precision.HIGH...  42.2 us
    pallas_call x1, Pallas kernels, reduce_grams(): pl.pallas_call(functools.partial(reduce_kernel, snap_count, cell_count, s...  24.8 us
    dot_general x4, matrix products, chunk_products(): jnp.einsum('rt,stc->rsc', wave_table[:, :half_len], segments[:-1], precis...  22.6 us
    dot_general x4, matrix products, chunk_products(): jnp.einsum('rt,stc->rsc', wave_table[:, half_len:], segments[1:], precisi...  21.5 us
    all_to_all x4, starting transfers between devices, on_device(): lax.all_to_all(shaped, 'snap', split_axis=1, concat_axis=0, tiled=True)  21.3 us
    reshape x4, local copies, waits for them, and re-layouts, on_device(): shaped = columns.reshape(row_count, snap_count, wide)  15.7 us
    unnamed x9, local copies, waits for them, and re-layouts  12.2 us
  transfers between devices with their start and end apart: 4, of which 4 were waited for; matrix products, arithmetic and copies ran while one was open for 18% of the time, Pallas kernels for 0%

profile of v2, /device:TPU:0, one launch (start us, length us, event | category | flops | bytes accessed | tf_op | source)
XLA Modules:
  0.0 472.8 jit_solution(1525918613841829503)
XLA Ops:
  0.0 11.2 %slice_bitcast_fusion = (f32[260,4,8,128]{3,2,1,0:T(8,128)}, f32[260,4,8,128]{3,2,1,0:T(8,128)}, f32[260,4,8,128]{3,2,1,0:T(8,128)}, f32[260,4,8,128]{3,2,1,0:T(8,128)S(1)}) fusion(f32[2080,2048]{1,0:T(8,128)} %param.3), kind=kLoop, calls=%fused_computation.4 | loop fusion | bytes 34078720
  11.2 2.3 copy.66
  13.5 6.4 %all-to-all-start.2 = ((f32[2080,4,128]{2,0,1:T(8,128)}), f32[2080,4,128]{2,0,1:T(8,128)}, u32[]{:S(2)}, u32[]{:S(2)}) async-start(f32[2080,4,128]{2,0,1:T(8,128)} %bitcast.105), calls=%async_computation.2 | async-start | bytes 8519680 | tf_op jit(solution)/shard_map/all_to_all | solution.py:152
  19.9 4.5 copy.68
  24.3 90.4 %all-to-all-done.2 = f32[2080,4,128]{2,0,1:T(8,128)} async-done(((f32[2080,4,128]{2,0,1:T(8,128)}), f32[2080,4,128]{2,0,1:T(8,128)}, u32[]{:S(2)}, u32[]{:S(2)}) %all-to-all-start.2) | async-done | bytes 4259872 | tf_op jit(solution)/shard_map/all_to_all | solution.py:152
  114.7 4.9 %all-to-all-start = ((f32[2080,4,128]{2,0,1:T(8,128)}), f32[2080,4,128]{2,0,1:T(8,128)}, u32[]{:S(2)}, u32[]{:S(2)}) async-start(f32[2080,4,128]{2,0,1:T(8,128)} %bitcast.104), calls=%async_computation | async-start | bytes 8519680 | tf_op jit(solution)/shard_map/all_to_all | solution.py:152
  119.6 4.5 copy.67
  124.1 89.5 %all-to-all-done = f32[2080,4,128]{2,0,1:T(8,128)} async-done(((f32[2080,4,128]{2,0,1:T(8,128)}), f32[2080,4,128]{2,0,1:T(8,128)}, u32[]{:S(2)}, u32[]{:S(2)}) %all-to-all-start) | async-done | bytes 4259872 | tf_op jit(solution)/shard_map/all_to_all | solution.py:152
  213.6 4.9 %all-to-all-start.1 = ((f32[2080,4,128]{2,0,1:T(8,128)}), f32[2080,4,128]{2,0,1:T(8,128)}, u32[]{:S(2)}, u32[]{:S(2)}) async-start(f32[2080,4,128]{2,0,1:T(8,128)} %bitcast.103), calls=%async_computation.1 | async-start | bytes 8519680 | tf_op jit(solution)/shard_map/all_to_all | solution.py:152
  218.5 4.5 copy.65
  223.0 89.7 %all-to-all-done.1 = f32[2080,4,128]{2,0,1:T(8,128)} async-done(((f32[2080,4,128]{2,0,1:T(8,128)}), f32[2080,4,128]{2,0,1:T(8,128)}, u32[]{:S(2)}, u32[]{:S(2)}) %all-to-all-start.1) | async-done | bytes 4259872 | tf_op jit(solution)/shard_map/all_to_all | solution.py:152
  312.7 5.2 %all-to-all-start.3 = ((f32[2080,4,128]{2,0,1:T(8,128)}), f32[2080,4,128]{2,0,1:T(8,128)}, u32[]{:S(2)}, u32[]{:S(2)}) async-start(f32[2080,4,128]{2,0,1:T(8,128)} %bitcast.102), calls=%async_computation.3 | async-start | bytes 8519680 | tf_op jit(solution)/shard_map/all_to_all | solution.py:152
  319.9 5.4 %fusion.4 = f32[128,64,128]{2,0,1:T(8,128)S(1)} fusion(f32[65,128,128]{2,1,0:T(8,128)} %bitcast.16, f32[128,256]{1,0:T(8,128)S(1)} %reshape.208), kind=kOutput, calls=%fused_computation.12 | convolution fusion | flops 1610612736 | bytes 8454144 | tf_op jit(solution)/shard_map/rt,stc->rsc/dot_general | solution.py:32
  325.3 5.4 %fusion.22 = f32[128,64,128]{2,0,1:T(8,128)S(1)} fusion(f32[128,64,128]{2,0,1:T(8,128)S(1)} %fusion.4, f32[65,128,128]{2,1,0:T(8,128)} %bitcast.16, f32[128,256]{1,0:T(8,128)S(1)} %reshape.208), kind=kOutput, calls=%fused_computation.27 | convolution fusion | flops 1611661312 | bytes 12648448 | tf_op jit(solution)/shard_map/rt,stc->rsc/dot_general | solution.py:31
  330.7 2.4 copy.44
  333.1 5.4 %fusion.12 = f32[128,64,128]{2,0,1:T(8,128)S(1)} fusion(f32[65,128,128]{2,1,0:T(8,128)} %bitcast.3, f32[128,256]{1,0:T(8,128)S(1)} %reshape.208), kind=kOutput, calls=%fused_computation.20 | convolution fusion | flops 1610612736 | bytes 8454144 | tf_op jit(solution)/shard_map/rt,stc->rsc/dot_general | solution.py:32
  338.5 6.1 %fusion.16 = f32[128,64,128]{2,0,1:T(8,128)S(1)} fusion(f32[128,64,128]{2,0,1:T(8,128)S(1)} %fusion.12, f32[65,128,128]{2,1,0:T(8,128)} %bitcast.3, f32[128,256]{1,0:T(8,128)S(1)} %reshape.208), kind=kOutput, calls=%fused_computation.25 | convolution fusion | flops 1611661312 | bytes 12648448 | tf_op jit(solution)/shard_map/rt,stc->rsc/dot_general | solution.py:31
  344.6 2.4 copy.40
  347.1 5.4 %fusion.8 = f32[128,64,128]{2,0,1:T(8,128)S(1)} fusion(f32[65,128,128]{2,1,0:T(8,128)} %bitcast.10, f32[128,256]{1,0:T(8,128)S(1)} %reshape.208), kind=kOutput, calls=%fused_computation.16 | convolution fusion | flops 1610612736 | bytes 8454144 | tf_op jit(solution)/shard_map/rt,stc->rsc/dot_general | solution.py:32
  352.5 5.7 %fusion.19 = f32[128,64,128]{2,0,1:T(8,128)S(1)} fusion(f32[128,64,128]{2,0,1:T(8,128)S(1)} %fusion.8, f32[65,128,128]{2,1,0:T(8,128)} %bitcast.10, f32[128,256]{1,0:T(8,128)S(1)} %reshape.208), kind=kOutput, calls=%fused_computation.26 | convolution fusion | flops 1611661312 | bytes 12648448 | tf_op jit(solution)/shard_map/rt,stc->rsc/dot_general | solution.py:31
  358.2 2.4 copy.42
  360.6 10.3 %fusion.49 = f32[64,128,128]{2,1,0:T(8,128)} fusion(f32[64,128,128]{2,1,0:T(8,128)S(1)} %bitcast.99), kind=kOutput, calls=%fused_computation.73 | convolution fusion | flops 1610612736 | bytes 8388608 | tf_op jit(solution)/shard_map/kbc,kdc->kbd/dot_general | solution.py:34
  370.9 10.5 %fusion.47 = f32[64,128,128]{2,1,0:T(8,128)} fusion(f32[64,128,128]{2,1,0:T(8,128)S(1)} %bitcast.100), kind=kOutput, calls=%fused_computation.71 | convolution fusion | flops 1610612736 | bytes 8388608 | tf_op jit(solution)/shard_map/kbc,kdc->kbd/dot_general | solution.py:34
  381.4 10.3 %fusion.48 = f32[64,128,128]{2,1,0:T(8,128)} fusion(f32[64,128,128]{2,1,0:T(8,128)S(1)} %bitcast.101), kind=kOutput, calls=%fused_computation.72 | convolution fusion | flops 1610612736 | bytes 8388608 | tf_op jit(solution)/shard_map/kbc,kdc->kbd/dot_general | solution.py:34
  391.7 20.3 %all-to-all-done.3 = f32[2080,4,128]{2,0,1:T(8,128)} async-done(((f32[2080,4,128]{2,0,1:T(8,128)}), f32[2080,4,128]{2,0,1:T(8,128)}, u32[]{:S(2)}, u32[]{:S(2)}) %all-to-all-start.3) | async-done | bytes 4259872 | tf_op jit(solution)/shard_map/all_to_all | solution.py:152
  412.0 5.4 %fusion = f32[128,64,128]{2,0,1:T(8,128)S(1)} fusion(f32[65,128,128]{2,1,0:T(8,128)} %bitcast.22, f32[128,256]{1,0:T(8,128)S(1)} %reshape.208), kind=kOutput, calls=%fused_computation.8 | convolution fusion | flops 1610612736 | bytes 8454144 | tf_op jit(solution)/shard_map/rt,stc->rsc/dot_general | solution.py:32
  417.4 5.4 %fusion.25 = f32[128,64,128]{2,0,1:T(8,128)S(1)} fusion(f32[128,64,128]{2,0,1:T(8,128)S(1)} %fusion, f32[65,128,128]{2,1,0:T(8,128)} %bitcast.22, f32[128,256]{1,0:T(8,128)S(1)} %reshape.208), kind=kOutput, calls=%fused_computation.28 | convolution fusion | flops 1611661312 | bytes 12648448 | tf_op jit(solution)/shard_map/rt,stc->rsc/dot_general | solution.py:31
  422.8 2.4 copy.46
  426.3 11.1 %add_add_fusion = f32[64,128,128]{2,1,0:T(8,128)S(1)} fusion(f32[64,128,128]{2,1,0:T(8,128)S(1)} %copy-done, f32[64,128,128]{2,1,0:T(8,128)S(1)} %copy-done.1, f32[64,128,128]{2,1,0:T(8,128)} %fusion.48, f32[64,128,128]{2,1,0:T(8,128)S(1)} %bitcast.98), kind=kOutput, calls=%fused_computation.24 | convolution fusion | flops 1613758464 | bytes 20971520 | tf_op jit(solution)/shard_map/kbc,kdc->kbd/dot_general | solution.py:34
  438.6 1.7 copy.69
  440.3 2.1 reshape.218
  442.4 24.8 %shard_map.37 = f32[8,64,128]{2,1,0:T(8,128)} custom-call(f32[8,4,64,128]{3,2,1,0:T(8,128)} %bitcast.108), custom_call_target="tpu_custom_call" | custom-call | tf_op jit(solution)/shard_map/pallas_call | solution.py:117
  (24 shorter events, 8.8 us)
Async XLA Ops:
  13.5 101.2 %all-to-all-start.2 = ((f32[2080,4,128]{2,0,1:T(8,128)}), f32[2080,4,128]{2,0,1:T(8,128)}, u32[]{:S(2)}, u32[]{:S(2)}) async-start(f32[2080,4,128]{2,0,1:T(8,128)} %bitcast.105), calls=%async_computation.2 | async-start | bytes 8519680 | tf_op jit(solution)/shard_map/all_to_all | solution.py:152
  114.7 99.0 %all-to-all-start = ((f32[2080,4,128]{2,0,1:T(8,128)}), f32[2080,4,128]{2,0,1:T(8,128)}, u32[]{:S(2)}, u32[]{:S(2)}) async-start(f32[2080,4,128]{2,0,1:T(8,128)} %bitcast.104), calls=%async_computation | async-start | bytes 8519680 | tf_op jit(solution)/shard_map/all_to_all | solution.py:152
  213.6 99.0 %all-to-all-start.1 = ((f32[2080,4,128]{2,0,1:T(8,128)}), f32[2080,4,128]{2,0,1:T(8,128)}, u32[]{:S(2)}, u32[]{:S(2)}) async-start(f32[2080,4,128]{2,0,1:T(8,128)} %bitcast.103), calls=%async_computation.1 | async-start | bytes 8519680 | tf_op jit(solution)/shard_map/all_to_all | solution.py:152
  312.7 6.6 %copy-start.2 = (s32[64]{0:T(128)S(1)}, s32[64]{0:T(128)}, u32[]{:S(2)}) copy-start(s32[64]{0:T(128)} %param.5) | copy-start | bytes 772
  312.7 7.2 %copy-start.3 = (s32[64]{0:T(128)S(1)}, s32[64]{0:T(128)}, u32[]{:S(2)}) copy-start(s32[64]{0:T(128)} %param.4) | copy-start | bytes 772
  312.7 99.4 %all-to-all-start.3 = ((f32[2080,4,128]{2,0,1:T(8,128)}), f32[2080,4,128]{2,0,1:T(8,128)}, u32[]{:S(2)}, u32[]{:S(2)}) async-start(f32[2080,4,128]{2,0,1:T(8,128)} %bitcast.102), calls=%async_computation.3 | async-start | bytes 8519680 | tf_op jit(solution)/shard_map/all_to_all | solution.py:152
  422.8 2.5 copy-start
  422.8 3.5 copy-start.1

commit v3 on v2

--- a/solution.py
+++ b/solution.py
@@ -9,7 +9,6 @@
 
 NFFT = 256
 LANES = 128
-MAX_CHUNKS = 4
 MESH = pl.DeviceIdType.MESH
 
 
@@ -25,13 +24,153 @@
     return wave_table.reshape(2 * retained_bins.shape[0], NFFT)
 
 
-def chunk_products(series, wave_table, kept_count, blocks):
+def gather_kernel(snap_count, chunks, wide, kept_count, blocks, pressure_ref, table_ref, out_ref, held, spectra, grams, table_parts,
+                  own_sem, send_sem, recv_sem):
+    my_snap, my_cell = lax.axis_index("snap"), lax.axis_index("cell")
+    row_count = pressure_ref.shape[0]
+    half_count = snap_count // 2
+    my_half = my_snap // half_count
     half_len = NFFT // 2
-    segments = series.reshape(series.shape[0] // half_len, half_len, series.shape[1])
-    front = jnp.einsum("rt,stc->rsc", wave_table[:, :half_len], segments[:-1], precision=lax.Precision.HIGHEST)
-    back = jnp.einsum("rt,stc->rsc", wave_table[:, half_len:], segments[1:], precision=lax.Precision.HIGHEST)
-    stacked = (front + back).reshape(kept_count, 2 * blocks, series.shape[1])
-    return jnp.einsum("kbc,kdc->kbd", stacked, stacked, precision=lax.Precision.HIGHEST)
+    near = [my_half * half_count + lax.rem(my_snap + step, half_count) for step in range(1, half_count)]
+    far = [(1 - my_half) * half_count + lax.rem(my_snap + step, half_count) for step in range(half_count)]
+
+    barrier = pltpu.get_barrier_semaphore()
+    for peer in near + far:
+        pl.semaphore_signal(barrier, inc=1, device_id=(peer, my_cell), device_id_type=MESH)
+    pl.semaphore_wait(barrier, snap_count - 1)
+
+    def columns(chunk, owner):
+        return pressure_ref.at[:, pl.ds(pl.multiple_of((chunk * snap_count + owner) * wide, wide), wide)]
+
+    def landing(chunk, source):
+        return held.at[chunk, pl.ds(pl.multiple_of(source * row_count, 8), row_count)]
+
+    def sending(chunk, peer):
+        return pltpu.make_async_remote_copy(
+            src_ref=columns(chunk, peer),
+            dst_ref=landing(chunk, my_snap),
+            send_sem=send_sem.at[chunk, peer],
+            recv_sem=recv_sem.at[chunk, my_snap],
+            device_id=(peer, my_cell),
+            device_id_type=MESH,
+        )
+
+    def arriving(chunk, peer):
+        return pltpu.make_async_remote_copy(
+            src_ref=columns(chunk, peer),
+            dst_ref=landing(chunk, peer),
+            send_sem=send_sem.at[chunk, peer],
+            recv_sem=recv_sem.at[chunk, peer],
+            device_id=(peer, my_cell),
+            device_id_type=MESH,
+        )
+
+    def keeping(chunk):
+        return pltpu.make_async_copy(columns(chunk, my_snap), landing(chunk, my_snap), own_sem.at[chunk])
+
+    for chunk in range(chunks):
+        for peer in near:
+            sending(chunk, peer).start()
+        keeping(chunk).start()
+    for chunk in range(chunks):
+        for peer in far:
+            sending(chunk, peer).start()
+
+    table = table_ref[...]
+    coarse = table.astype(jnp.bfloat16)
+    rows_out = 2 * kept_count
+    table_parts[:rows_out] = coarse
+    table_parts[rows_out:] = (table - coarse.astype(jnp.float32)).astype(jnp.bfloat16)
+
+    half_rows = snap_count * row_count // 2
+    low_count = (half_rows - NFFT) // half_len + 1
+    high_start = -(-half_rows // half_len)
+    high_count = blocks - high_start
+
+    def transform(chunk, first, count):
+        def body(step, carry):
+            block = first + step
+            data = held[chunk, pl.ds(pl.multiple_of(block * half_len, half_len), NFFT), :]
+            data_coarse = data.astype(jnp.bfloat16)
+            data_fine = (data - data_coarse.astype(jnp.float32)).astype(jnp.bfloat16)
+            both = jnp.dot(table_parts[...], data_coarse, preferred_element_type=jnp.float32)
+            rest = jnp.dot(table_parts[:rows_out], data_fine, preferred_element_type=jnp.float32)
+            spectra[pl.ds(block, rows_out, stride=blocks), :] = both[:rows_out] + (both[rows_out:] + rest)
+            return carry
+
+        lax.fori_loop(0, count, body, 0, unroll=False)
+
+    def product(k):
+        data = spectra[pl.ds(pl.multiple_of(k * 2 * blocks, 2 * blocks), 2 * blocks), :]
+        data_coarse = data.astype(jnp.bfloat16)
+        data_fine = (data - data_coarse.astype(jnp.float32)).astype(jnp.bfloat16)
+        left = jnp.concatenate([data_coarse, data_coarse, data_fine], 1)
+        right = jnp.concatenate([data_coarse, data_fine, data_coarse], 1)
+        return lax.dot_general(left, right, (((1,), (1,)), ((), ())), preferred_element_type=jnp.float32)
+
+    def complex_gram(k):
+        whole = grams[k] + product(k) if chunks > 1 else product(k)
+        top, turned = whole[:blocks], pltpu.roll(whole[blocks:], blocks, 1)
+        lane = lax.broadcasted_iota(jnp.int32, top.shape, 1)
+        return jnp.where(lane < blocks, top + turned, top - turned)
+
+    for chunk in range(chunks):
+        keeping(chunk).wait()
+        for peer in near:
+            arriving(chunk, peer).wait_recv()
+        transform(chunk, my_half * high_start, low_count + my_half * (high_count - low_count))
+        for peer in far:
+            arriving(chunk, peer).wait_recv()
+        transform(chunk, low_count, high_start - low_count)
+        transform(chunk, (1 - my_half) * high_start, high_count + my_half * (low_count - high_count))
+        if chunk < chunks - 1:
+            def accumulate(k, carry, chunk=chunk):
+                grams[k] = product(k) if chunk == 0 else grams[k] + product(k)
+                return carry
+
+            lax.fori_loop(0, kept_count, accumulate, 0, unroll=False)
+
+    pairs = kept_count // snap_count // 2
+
+    def finish(place, carry):
+        k = place // pairs * (2 * pairs) + lax.rem(place, pairs)
+        first, second = complex_gram(k), complex_gram(k + pairs)
+        row = lax.broadcasted_iota(jnp.int32, first.shape, 0)
+        lane = lax.broadcasted_iota(jnp.int32, first.shape, 1)
+        left = jnp.where(row >= lane, first, pltpu.roll(first, blocks, 1))
+        right = jnp.where(row >= lane - blocks, pltpu.roll(second, blocks, 1), second)
+        out_ref[place] = jnp.where(lane < blocks, left, right)
+        return carry
+
+    lax.fori_loop(0, kept_count // 2, finish, 0, unroll=False)
+    for chunk in range(chunks):
+        for peer in near + far:
+            sending(chunk, peer).wait_send()
+
+
+def local_grams(pressure, wave_table, snap_count, blocks):
+    row_count, width_local = pressure.shape
+    pieces = width_local // snap_count
+    wide = LANES
+    chunks = pieces // wide
+    kept_count = wave_table.shape[0] // 2
+    whole_vmem = pl.BlockSpec(memory_space=pltpu.VMEM)
+    return pl.pallas_call(
+        functools.partial(gather_kernel, snap_count, chunks, wide, kept_count, blocks),
+        out_shape=jax.ShapeDtypeStruct((kept_count // 2, blocks, 2 * blocks), jnp.float32),
+        in_specs=[pl.BlockSpec(memory_space=pl.ANY), whole_vmem],
+        out_specs=whole_vmem,
+        scratch_shapes=[
+            pltpu.VMEM((chunks, snap_count * row_count, wide), jnp.float32),
+            pltpu.VMEM((2 * kept_count * blocks, wide), jnp.float32),
+            pltpu.VMEM((kept_count, 2 * blocks, 2 * blocks), jnp.float32),
+            pltpu.VMEM((4 * kept_count, NFFT), jnp.bfloat16),
+            pltpu.SemaphoreType.DMA((chunks,)),
+            pltpu.SemaphoreType.DMA((chunks, snap_count)),
+            pltpu.SemaphoreType.DMA((chunks, snap_count)),
+        ],
+        compiler_params=pltpu.CompilerParams(collective_id=1, has_side_effects=True),
+    )(pressure, wave_table)
 
 
 def reduce_kernel(snap_count, cell_count, scale, gram_ref, out_ref, cell_slots, own_cells, snap_slots, own_part, gathered,
@@ -53,7 +192,7 @@
 
     scatters = [
         pltpu.make_async_remote_copy(
-            src_ref=gram_ref.at[cell_peer(step)],
+            src_ref=gram_ref.at[:, cell_peer(step)],
             dst_ref=cell_slots.at[step - 1],
             send_sem=cell_send.at[step - 1],
             recv_sem=cell_recv.at[step - 1],
@@ -64,7 +203,7 @@
     ]
     for copy in scatters:
         copy.start()
-    total = gram_ref[my_cell]
+    total = gram_ref[:, my_cell]
     for step in range(1, cell_count):
         scatters[step - 1].wait_recv()
         total = total + cell_slots[step - 1]
@@ -112,7 +251,7 @@
 
 
 def reduce_grams(packed, scale):
-    cell_count, snap_count, rows, lanes = packed.shape
+    snap_count, cell_count, rows, lanes = packed.shape
     whole_vmem = pl.BlockSpec(memory_space=pltpu.VMEM)
     return pl.pallas_call(
         functools.partial(reduce_kernel, snap_count, cell_count, scale),
@@ -139,29 +278,14 @@
 def on_device(pressure, block_starts, retained_bins):
     snap_count = lax.axis_size("snap")
     row_count, width_local = pressure.shape
-    pieces = width_local // snap_count
-    chunks = max(n for n in range(1, MAX_CHUNKS + 1) if pieces % (n * LANES) == 0)
-    wide = pieces // chunks
-    wave_table = make_table(retained_bins)
     kept_count = retained_bins.shape[0]
     blocks = block_starts.shape[0]
-    received = []
-    for i in range(chunks):
-        columns = pressure[:, i * snap_count * wide:(i + 1) * snap_count * wide]
-        shaped = columns.reshape(row_count, snap_count, wide)
-        received.append(lax.all_to_all(shaped, "snap", split_axis=1, concat_axis=0, tiled=True)[:, 0, :])
-    products = chunk_products(received[0], wave_table, kept_count, blocks)
-    for series in received[1:]:
-        products = products + chunk_products(series, wave_table, kept_count, blocks)
-    real_part = products[:, :blocks, :blocks] + products[:, blocks:, blocks:]
-    imag_part = products[:, :blocks, blocks:] - products[:, blocks:, :blocks]
+    halves = local_grams(pressure, make_table(retained_bins), snap_count, blocks)
     lower = jnp.arange(blocks)[:, None] >= jnp.arange(blocks)[None, :]
-    halves = jnp.where(lower, real_part, imag_part)
     cell_count = lax.axis_size("cell")
     pairs = kept_count // snap_count // 2
     rows = pairs * blocks // cell_count
-    split = halves.reshape(snap_count, 2, pairs, blocks, blocks).transpose(0, 2, 3, 1, 4)
-    packed = split.reshape(snap_count, cell_count, rows, 2 * blocks).transpose(1, 0, 2, 3)
+    packed = halves.reshape(snap_count, cell_count, rows, 2 * blocks)
     reduced = reduce_grams(packed, 1.0 / (width_local * cell_count))
     joined = reduced.reshape(pairs, blocks, 2, blocks).transpose(2, 0, 1, 3).reshape(2 * pairs, blocks, blocks)
     mirrored = joined.transpose(0, 2, 1)

time: 476 us -> 427 us (0.90)
  Pallas kernels: 24.8 us -> 418 us
  waiting for transfers between devices: 290 us -> 0 us
  matrix products: 88.6 us -> 2.29 us
  local copies, waits for them, and re-layouts: 44.5 us -> 3.69 us
  starting transfers between devices: 21.3 us -> 0 us
    pallas_call x0 -> x1, Pallas kernels: none -> 372 us  [local_grams(): pl.pallas_call(functools.partial(gather_kernel, snap_count, chunks, wide,...]
    all_to_all x4 -> x0, waiting for transfers between devices: 290 us -> none  [on_device(): lax.all_to_all(shaped, 'snap', split_axis=1, concat_axis=0, tiled=True)]
    dot_general x12 -> x0, matrix products: 86.3 us -> none  [the longest x4 42.2 us: chunk_products(): jnp.einsum('kbc,kdc->kbd', stacked, stacked, precision=lax.Precision.HIGH...]
    pallas_call x1, Pallas kernels: 24.8 us -> 46.2 us  [reduce_grams(): pl.pallas_call(functools.partial(reduce_kernel, snap_count, cell_count, s...]
    all_to_all x4 -> x0, starting transfers between devices: 21.3 us -> none  [on_device(): lax.all_to_all(shaped, 'snap', split_axis=1, concat_axis=0, tiled=True)]
    reshape x6 -> x0, local copies, waits for them, and re-layouts: 19.5 us -> none  [the longest x4 15.7 us: on_device(): shaped = columns.reshape(row_count, snap_count, wide)]
    unnamed x9 -> x2, local copies, waits for them, and re-layouts: 12.2 us -> 0.01 us
    add x4 -> x0, local copies, waits for them, and re-layouts: 9.72 us -> none  [chunk_products(): stacked = (front + back).reshape(kept_count, 2 * blocks, series.shape[1])]
  transfers between devices with their start and end apart: 4 -> 0, of which waited for: 4 -> 0; matrix products, arithmetic and copies ran while one was open for 18% -> 0% of each run, Pallas kernels for 0% -> 0%
where the time goes in v3:
time: 427 us
  Pallas kernels  418 us (98%)
    pallas_call x1, Pallas kernels, local_grams(): pl.pallas_call(functools.partial(gather_kernel, snap_count, chunks, wide,...  372 us
    pallas_call x1, Pallas kernels, reduce_grams(): pl.pallas_call(functools.partial(reduce_kernel, snap_count, cell_count, s...  46.2 us

profile of v3, /device:TPU:0, one launch (start us, length us, event | category | flops | bytes accessed | tf_op | source)
XLA Modules:
  0.0 427.1 jit_solution(403280184017919412)
XLA Ops:
  0.0 0.0 copy-start
  0.0 0.6 multiply_reduce_fusion
  1.4 1.0 cosine_multiply_fusion
  2.4 0.1 copy.10
  2.5 0.7 reshape.177.table_ref
  3.3 372.3 %shard_map.37 = f32[32,64,128]{2,1,0:T(8,128)} custom-call(f32[2080,2048]{1,0:T(8,128)} %pressure_ref.1, f32[128,256]{1,0:T(8,128)} %reshape.177.table_ref), custom_call_target="tpu_custom_call" | custom-call | tf_op jit(solution)/shard_map/pallas_call | solution.py:158
  375.5 46.2 %shard_map.38 = f32[8,64,128]{2,1,0:T(8,128)} custom-call(f32[4,8,64,128]{3,2,1,0:T(8,128)} %bitcast.28), custom_call_target="tpu_custom_call" | custom-call | tf_op jit(solution)/shard_map/pallas_call | solution.py:256
  421.7 1.3 reshape.179
  423.1 0.2 copy.18
  423.3 0.2 bitcast_select_fusion
  423.5 0.0 copy-done
  423.5 1.6 fusion
  425.1 0.7 convolution_bitcast_fusion
  425.8 1.3 copy.15
  (5 shorter events, 0.1 us)
Async XLA Ops:
  0.0 423.5 %copy-start = (s32[64]{0:T(128)S(1)}, s32[64]{0:T(128)}, u32[]{:S(2)}) copy-start(s32[64]{0:T(128)} %param.4) | copy-start | bytes 772

commit v4 on v3

--- a/solution.py
+++ b/solution.py
@@ -18,14 +18,22 @@
     norm_factor = 1.0 / jnp.sqrt(jnp.sum(window * window))
     phase_steps = retained_bins[:, None] * offsets[None, :] % NFFT
     angles = 2.0 * jnp.pi * phase_steps.astype(jnp.float32) / NFFT
-    wave_table = jnp.stack(
-        [window * norm_factor * jnp.cos(angles), -window * norm_factor * jnp.sin(angles)], 1
-    )
-    return wave_table.reshape(2 * retained_bins.shape[0], NFFT)
-
-
-def gather_kernel(snap_count, chunks, wide, kept_count, blocks, pressure_ref, table_ref, out_ref, held, spectra, grams, table_parts,
-                  own_sem, send_sem, recv_sem):
+    return jnp.concatenate([window * norm_factor * jnp.cos(angles), -window * norm_factor * jnp.sin(angles)], 0)
+
+
+def repeat(count, unroll, step):
+    def body(turn, carry):
+        for extra in range(unroll):
+            step(turn * unroll + extra)
+        return carry
+
+    lax.fori_loop(0, count // unroll, body, 0)
+    for rest in range(count // unroll * unroll, count):
+        step(rest)
+
+
+def gather_kernel(snap_count, cell_count, chunks, wide, kept_count, blocks, scale, pressure_ref, table_ref, out_ref, held, spectra, grams,
+                  table_parts, own_sem, send_sem, recv_sem, *reduction):
     my_snap, my_cell = lax.axis_index("snap"), lax.axis_index("cell")
     row_count = pressure_ref.shape[0]
     half_count = snap_count // 2
@@ -37,7 +45,10 @@
     barrier = pltpu.get_barrier_semaphore()
     for peer in near + far:
         pl.semaphore_signal(barrier, inc=1, device_id=(peer, my_cell), device_id_type=MESH)
-    pl.semaphore_wait(barrier, snap_count - 1)
+    if reduction:
+        for step in range(1, cell_count):
+            pl.semaphore_signal(barrier, inc=1, device_id=(my_snap, lax.rem(my_cell + step, cell_count)), device_id_type=MESH)
+    pl.semaphore_wait(barrier, snap_count + cell_count - 2 if reduction else snap_count - 1)
 
     def columns(chunk, owner):
         return pressure_ref.at[:, pl.ds(pl.multiple_of((chunk * snap_count + owner) * wide, wide), wide)]
@@ -85,23 +96,29 @@
     half_rows = snap_count * row_count // 2
     low_count = (half_rows - NFFT) // half_len + 1
     high_start = -(-half_rows // half_len)
-    high_count = blocks - high_start
+    assert low_count == blocks - high_start
 
     def transform(chunk, first, count):
-        def body(step, carry):
-            block = first + step
-            data = held[chunk, pl.ds(pl.multiple_of(block * half_len, half_len), NFFT), :]
+        def spread(block, width):
+            data = jnp.concatenate(
+                [held[chunk, pl.ds(pl.multiple_of((block + i) * half_len, half_len), NFFT), :] for i in range(width)], 1
+            )
             data_coarse = data.astype(jnp.bfloat16)
             data_fine = (data - data_coarse.astype(jnp.float32)).astype(jnp.bfloat16)
             both = jnp.dot(table_parts[...], data_coarse, preferred_element_type=jnp.float32)
             rest = jnp.dot(table_parts[:rows_out], data_fine, preferred_element_type=jnp.float32)
-            spectra[pl.ds(block, rows_out, stride=blocks), :] = both[:rows_out] + (both[rows_out:] + rest)
-            return carry
-
-        lax.fori_loop(0, count, body, 0, unroll=False)
+            result = both[:rows_out] + (both[rows_out:] + rest)
+            for i in range(width):
+                spectra[pl.ds(block + i, rows_out, stride=blocks), :] = result[:, i * wide:(i + 1) * wide]
+
+        repeat(count // 2, 2, lambda step: spread(first + 2 * step, 2))
+        if count % 2:
+            spread(first + count - 1, 1)
 
     def product(k):
-        data = spectra[pl.ds(pl.multiple_of(k * 2 * blocks, 2 * blocks), 2 * blocks), :]
+        data = jnp.concatenate(
+            [spectra[pl.ds(pl.multiple_of((k + part * kept_count) * blocks, blocks), blocks), :] for part in range(2)], 0
+        )
         data_coarse = data.astype(jnp.bfloat16)
         data_fine = (data - data_coarse.astype(jnp.float32)).astype(jnp.bfloat16)
         left = jnp.concatenate([data_coarse, data_coarse, data_fine], 1)
@@ -118,46 +135,147 @@
         keeping(chunk).wait()
         for peer in near:
             arriving(chunk, peer).wait_recv()
-        transform(chunk, my_half * high_start, low_count + my_half * (high_count - low_count))
+        transform(chunk, my_half * high_start, low_count)
         for peer in far:
             arriving(chunk, peer).wait_recv()
         transform(chunk, low_count, high_start - low_count)
-        transform(chunk, (1 - my_half) * high_start, high_count + my_half * (low_count - high_count))
+        transform(chunk, (1 - my_half) * high_start, low_count)
         if chunk < chunks - 1:
-            def accumulate(k, carry, chunk=chunk):
+            def accumulate(k, chunk=chunk):
                 grams[k] = product(k) if chunk == 0 else grams[k] + product(k)
-                return carry
-
-            lax.fori_loop(0, kept_count, accumulate, 0, unroll=False)
+
+            repeat(kept_count, 4, accumulate)
 
     pairs = kept_count // snap_count // 2
 
-    def finish(place, carry):
+    def finish(place):
         k = place // pairs * (2 * pairs) + lax.rem(place, pairs)
         first, second = complex_gram(k), complex_gram(k + pairs)
         row = lax.broadcasted_iota(jnp.int32, first.shape, 0)
         lane = lax.broadcasted_iota(jnp.int32, first.shape, 1)
         left = jnp.where(row >= lane, first, pltpu.roll(first, blocks, 1))
         right = jnp.where(row >= lane - blocks, pltpu.roll(second, blocks, 1), second)
-        out_ref[place] = jnp.where(lane < blocks, left, right)
-        return carry
-
-    lax.fori_loop(0, kept_count // 2, finish, 0, unroll=False)
+        return jnp.where(lane < blocks, left, right)
+
+    if not reduction:
+        def write(place):
+            out_ref[place] = finish(place)
+
+        repeat(kept_count // 2, 2, write)
+    else:
+        reduce_places(snap_count, cell_count, scale, pairs, blocks, finish, out_ref, *reduction)
     for chunk in range(chunks):
         for peer in near + far:
             sending(chunk, peer).wait_send()
 
 
-def local_grams(pressure, wave_table, snap_count, blocks):
+def reduce_places(snap_count, cell_count, scale, pairs, blocks, finish, out_ref, packed, cell_slots, own_cells, snap_slots, own_part,
+                  gathered, cell_send, cell_recv, snap_send, snap_recv, gather_send, gather_recv):
+    my_snap, my_cell = lax.axis_index("snap"), lax.axis_index("cell")
+    rows = own_part.shape[0]
+
+    def cell_peer(step):
+        return lax.rem(my_cell + step, cell_count)
+
+    def owner(turn):
+        return lax.rem(my_snap + turn + 1, snap_count)
+
+    def share(cell):
+        return pl.ds(pl.multiple_of(cell * rows, 8), rows)
+
+    def scattering(turn, step):
+        return pltpu.make_async_remote_copy(
+            src_ref=packed.at[owner(turn), share(cell_peer(step))],
+            dst_ref=cell_slots.at[step - 1, turn],
+            send_sem=cell_send.at[step - 1, turn],
+            recv_sem=cell_recv.at[step - 1, turn],
+            device_id=(my_snap, cell_peer(step)),
+            device_id_type=MESH,
+        )
+
+    def exchanging(turn):
+        return pltpu.make_async_remote_copy(
+            src_ref=own_cells.at[turn],
+            dst_ref=snap_slots.at[turn],
+            send_sem=snap_send.at[turn],
+            recv_sem=snap_recv.at[turn],
+            device_id=(owner(turn), my_cell),
+            device_id_type=MESH,
+        )
+
+    def gathering(step):
+        return pltpu.make_async_remote_copy(
+            src_ref=own_part,
+            dst_ref=gathered.at[step - 1],
+            send_sem=gather_send.at[step - 1],
+            recv_sem=gather_recv.at[step - 1],
+            device_id=(my_snap, cell_peer(step)),
+            device_id_type=MESH,
+        )
+
+    for turn in range(snap_count):
+        def write(pair, turn=turn):
+            packed[owner(turn), pl.ds(pl.multiple_of(pair * blocks, blocks), blocks)] = finish(owner(turn) * pairs + pair)
+
+        repeat(pairs, 2, write)
+        for step in range(1, cell_count):
+            scattering(turn, step).start()
+    for turn in range(snap_count):
+        total = packed[owner(turn), share(my_cell)]
+        for step in range(1, cell_count):
+            scattering(turn, step).wait_recv()
+            total = total + cell_slots[step - 1, turn]
+        own_cells[turn] = total
+        if turn < snap_count - 1:
+            exchanging(turn).start()
+    part = own_cells[snap_count - 1]
+    for turn in range(snap_count - 1):
+        exchanging(turn).wait_recv()
+        part = part + snap_slots[turn]
+    own_part[...] = part * scale
+    for step in range(1, cell_count):
+        gathering(step).start()
+    out_ref[my_cell] = own_part[...]
+    for step in range(1, cell_count):
+        gathering(step).wait_recv()
+        out_ref[lax.rem(my_cell + cell_count - step, cell_count)] = gathered[step - 1]
+    for step in range(1, cell_count):
+        gathering(step).wait_send()
+        for turn in range(snap_count):
+            scattering(turn, step).wait_send()
+    for turn in range(snap_count - 1):
+        exchanging(turn).wait_send()
+
+
+def local_grams(pressure, wave_table, snap_count, cell_count, blocks, reduced_rows):
     row_count, width_local = pressure.shape
     pieces = width_local // snap_count
     wide = LANES
     chunks = pieces // wide
     kept_count = wave_table.shape[0] // 2
     whole_vmem = pl.BlockSpec(memory_space=pltpu.VMEM)
+    lanes = 2 * blocks
+    out_shape, extra = (kept_count // 2, blocks, lanes), []
+    if reduced_rows:
+        out_shape = (cell_count, reduced_rows, lanes)
+        extra = [
+            pltpu.VMEM((snap_count, cell_count * reduced_rows, lanes), jnp.float32),
+            pltpu.VMEM((cell_count - 1, snap_count, reduced_rows, lanes), jnp.float32),
+            pltpu.VMEM((snap_count, reduced_rows, lanes), jnp.float32),
+            pltpu.VMEM((snap_count - 1, reduced_rows, lanes), jnp.float32),
+            pltpu.VMEM((reduced_rows, lanes), jnp.float32),
+            pltpu.VMEM((cell_count - 1, reduced_rows, lanes), jnp.float32),
+            pltpu.SemaphoreType.DMA((cell_count - 1, snap_count)),
+            pltpu.SemaphoreType.DMA((cell_count - 1, snap_count)),
+            pltpu.SemaphoreType.DMA((snap_count - 1,)),
+            pltpu.SemaphoreType.DMA((snap_count - 1,)),
+            pltpu.SemaphoreType.DMA((cell_count - 1,)),
+            pltpu.SemaphoreType.DMA((cell_count - 1,)),
+        ]
+    scale = 1.0 / (width_local * cell_count)
     return pl.pallas_call(
-        functools.partial(gather_kernel, snap_count, chunks, wide, kept_count, blocks),
-        out_shape=jax.ShapeDtypeStruct((kept_count // 2, blocks, 2 * blocks), jnp.float32),
+        functools.partial(gather_kernel, snap_count, cell_count, chunks, wide, kept_count, blocks, scale),
+        out_shape=jax.ShapeDtypeStruct(out_shape, jnp.float32),
         in_specs=[pl.BlockSpec(memory_space=pl.ANY), whole_vmem],
         out_specs=whole_vmem,
         scratch_shapes=[
@@ -168,6 +286,7 @@
             pltpu.SemaphoreType.DMA((chunks,)),
             pltpu.SemaphoreType.DMA((chunks, snap_count)),
             pltpu.SemaphoreType.DMA((chunks, snap_count)),
+            *extra,
         ],
         compiler_params=pltpu.CompilerParams(collective_id=1, has_side_effects=True),
     )(pressure, wave_table)
@@ -280,13 +399,17 @@
     row_count, width_local = pressure.shape
     kept_count = retained_bins.shape[0]
     blocks = block_starts.shape[0]
-    halves = local_grams(pressure, make_table(retained_bins), snap_count, blocks)
     lower = jnp.arange(blocks)[:, None] >= jnp.arange(blocks)[None, :]
     cell_count = lax.axis_size("cell")
     pairs = kept_count // snap_count // 2
     rows = pairs * blocks // cell_count
-    packed = halves.reshape(snap_count, cell_count, rows, 2 * blocks)
-    reduced = reduce_grams(packed, 1.0 / (width_local * cell_count))
+    wave_table = make_table(retained_bins)
+    if rows % 8 == 0:
+        reduced = local_grams(pressure, wave_table, snap_count, cell_count, blocks, rows)
+    else:
+        halves = local_grams(pressure, wave_table, snap_count, cell_count, blocks, 0)
+        packed = halves.reshape(snap_count, cell_count, rows, 2 * blocks)
+        reduced = reduce_grams(packed, 1.0 / (width_local * cell_count))
     joined = reduced.reshape(pairs, blocks, 2, blocks).transpose(2, 0, 1, 3).reshape(2 * pairs, blocks, blocks)
     mirrored = joined.transpose(0, 2, 1)
     diagonal = jnp.eye(blocks, dtype=bool)

time: 427 us -> 408 us (0.956)
  Pallas kernels: 418 us -> 399 us
    pallas_call x2 -> x1, Pallas kernels: 418 us -> 399 us  [local_grams(): pl.pallas_call(functools.partial(gather_kernel, snap_count, cell_count, c...]
where the time goes in v4:
time: 408 us
  Pallas kernels  399 us (98%)
    pallas_call x1, Pallas kernels, local_grams(): pl.pallas_call(functools.partial(gather_kernel, snap_count, cell_count, c...  399 us

profile of v4, /device:TPU:0, one launch (start us, length us, event | category | flops | bytes accessed | tf_op | source)
XLA Modules:
  0.0 407.9 jit_solution(4604842523102961477)
XLA Ops:
  0.0 0.0 copy-start
  0.0 0.6 multiply_reduce_fusion
  1.4 1.0 cosine_multiply_fusion
  2.4 0.7 pad_maximum_fusion.1.table_ref
  3.1 399.5 %shard_map.37 = f32[8,64,128]{2,1,0:T(8,128)} custom-call(f32[2080,2048]{1,0:T(8,128)} %pressure_ref.1, f32[128,256]{1,0:T(8,128)} %pad_maximum_fusion.1.table_ref), custom_call_target="tpu_custom_call" | custom-call | tf_op jit(solution)/shard_map/pallas_call | solution.py:276
  402.5 1.3 reshape.39
  403.8 0.2 copy.12
  404.0 0.1 copy.7
  404.1 0.2 bitcast_select_fusion
  404.3 0.0 copy-done
  404.3 1.6 fusion
  405.9 0.7 convolution_bitcast_fusion
  406.6 1.3 copy.9
  (3 shorter events, 0.1 us)
Async XLA Ops:
  0.0 404.3 %copy-start = (s32[64]{0:T(128)S(1)}, s32[64]{0:T(128)}, u32[]{:S(2)}) copy-start(s32[64]{0:T(128)} %param.4) | copy-start | bytes 772

commit v5 on v4

--- a/solution.py
+++ b/solution.py
@@ -12,13 +12,13 @@
 MESH = pl.DeviceIdType.MESH
 
 
-def make_table(retained_bins):
-    offsets = jnp.arange(NFFT, dtype=jnp.int32)
+def make_table(bins):
+    offsets = lax.broadcasted_iota(jnp.int32, (NFFT, bins.shape[1]), 0)
     window = 0.5 - 0.5 * jnp.cos(2.0 * jnp.pi * offsets.astype(jnp.float32) / NFFT)
-    norm_factor = 1.0 / jnp.sqrt(jnp.sum(window * window))
-    phase_steps = retained_bins[:, None] * offsets[None, :] % NFFT
+    norm_factor = 1.0 / jnp.sqrt(jnp.sum(window * window, axis=0, keepdims=True))
+    phase_steps = (bins * offsets) & (NFFT - 1)
     angles = 2.0 * jnp.pi * phase_steps.astype(jnp.float32) / NFFT
-    return jnp.concatenate([window * norm_factor * jnp.cos(angles), -window * norm_factor * jnp.sin(angles)], 0)
+    return jnp.concatenate([window * norm_factor * jnp.cos(angles), -window * norm_factor * jnp.sin(angles)], 1)
 
 
 def repeat(count, unroll, step):
@@ -32,7 +32,7 @@
         step(rest)
 
 
-def gather_kernel(snap_count, cell_count, chunks, wide, kept_count, blocks, scale, pressure_ref, table_ref, out_ref, held, spectra, grams,
+def gather_kernel(snap_count, cell_count, chunks, wide, kept_count, blocks, scale, pressure_ref, bins_ref, out_ref, held, spectra, grams,
                   table_parts, own_sem, send_sem, recv_sem, *reduction):
     my_snap, my_cell = lax.axis_index("snap"), lax.axis_index("cell")
     row_count = pressure_ref.shape[0]
@@ -87,7 +87,7 @@
         for peer in far:
             sending(chunk, peer).start()
 
-    table = table_ref[...]
+    table = make_table(bins_ref[...]).T
     coarse = table.astype(jnp.bfloat16)
     rows_out = 2 * kept_count
     table_parts[:rows_out] = coarse
@@ -247,12 +247,12 @@
         exchanging(turn).wait_send()
 
 
-def local_grams(pressure, wave_table, snap_count, cell_count, blocks, reduced_rows):
+def local_grams(pressure, retained_bins, snap_count, cell_count, blocks, reduced_rows):
     row_count, width_local = pressure.shape
     pieces = width_local // snap_count
     wide = LANES
     chunks = pieces // wide
-    kept_count = wave_table.shape[0] // 2
+    kept_count = retained_bins.shape[0]
     whole_vmem = pl.BlockSpec(memory_space=pltpu.VMEM)
     lanes = 2 * blocks
     out_shape, extra = (kept_count // 2, blocks, lanes), []
@@ -289,7 +289,7 @@
             *extra,
         ],
         compiler_params=pltpu.CompilerParams(collective_id=1, has_side_effects=True),
-    )(pressure, wave_table)
+    )(pressure, retained_bins.reshape(1, kept_count))
 
 
 def reduce_kernel(snap_count, cell_count, scale, gram_ref, out_ref, cell_slots, own_cells, snap_slots, own_part, gathered,
@@ -403,14 +403,14 @@
     cell_count = lax.axis_size("cell")
     pairs = kept_count // snap_count // 2
     rows = pairs * blocks // cell_count
-    wave_table = make_table(retained_bins)
     if rows % 8 == 0:
-        reduced = local_grams(pressure, wave_table, snap_count, cell_count, blocks, rows)
+        reduced = local_grams(pressure, retained_bins, snap_count, cell_count, blocks, rows)
     else:
-        halves = local_grams(pressure, wave_table, snap_count, cell_count, blocks, 0)
+        halves = local_grams(pressure, retained_bins, snap_count, cell_count, blocks, 0)
         packed = halves.reshape(snap_count, cell_count, rows, 2 * blocks)
         reduced = reduce_grams(packed, 1.0 / (width_local * cell_count))
-    joined = reduced.reshape(pairs, blocks, 2, blocks).transpose(2, 0, 1, 3).reshape(2 * pairs, blocks, blocks)
+    paired = reduced.reshape(pairs, blocks, 2 * blocks)
+    joined = jnp.concatenate([paired[:, :, :blocks], paired[:, :, blocks:]], 0)
     mirrored = joined.transpose(0, 2, 1)
     diagonal = jnp.eye(blocks, dtype=bool)
     own_real = jnp.where(lower, joined, mirrored)

time: 408 us -> 405 us (level)
  no operation moved by 1% of the time
where the time goes in v5:
time: 405 us
  Pallas kernels  399 us (99%)
    pallas_call x1, Pallas kernels, local_grams(): pl.pallas_call(functools.partial(gather_kernel, snap_count, cell_count, c...  399 us

profile of v5, /device:TPU:0, one launch (start us, length us, event | category | flops | bytes accessed | tf_op | source)
XLA Modules:
  0.0 405.1 jit_solution(11201347702029583606)
XLA Ops:
  0.0 0.7 and_select_fusion
  0.7 399.2 %shard_map.37 = f32[8,64,128]{2,1,0:T(8,128)} custom-call(f32[2080,2048]{1,0:T(8,128)} %pressure_ref.1, s32[1,64]{1,0:T(1,128)} %bitcast.25), custom_call_target="tpu_custom_call" | custom-call | tf_op jit(solution)/shard_map/pallas_call | solution.py:276
  399.9 1.2 fusion.11
  401.1 0.2 copy.4
  401.3 0.2 fusion.2
  401.5 1.6 fusion
  403.2 0.7 convolution_bitcast_fusion
  403.8 1.3 copy.5
  (2 shorter events, 0.1 us)

commit v6 on v5

--- a/solution.py
+++ b/solution.py
@@ -121,9 +121,10 @@
         )
         data_coarse = data.astype(jnp.bfloat16)
         data_fine = (data - data_coarse.astype(jnp.float32)).astype(jnp.bfloat16)
-        left = jnp.concatenate([data_coarse, data_coarse, data_fine], 1)
-        right = jnp.concatenate([data_coarse, data_fine, data_coarse], 1)
-        return lax.dot_general(left, right, (((1,), (1,)), ((), ())), preferred_element_type=jnp.float32)
+        right = jnp.concatenate([data_coarse, data_fine], 0)
+        both = lax.dot_general(data_coarse, right, (((1,), (1,)), ((), ())), preferred_element_type=jnp.float32)
+        cross = both[:, 2 * blocks:]
+        return both[:, :2 * blocks] + (cross + cross.T)
 
     def complex_gram(k):
         whole = grams[k] + product(k) if chunks > 1 else product(k)

time: 405 us -> 405 us (level)
  no operation moved by 1% of the time
where the time goes in v6:
time: 405 us
  Pallas kernels  399 us (99%)
    pallas_call x1, Pallas kernels, local_grams(): pl.pallas_call(functools.partial(gather_kernel, snap_count, cell_count, c...  399 us

profile of v6, /device:TPU:0, one launch (start us, length us, event | category | flops | bytes accessed | tf_op | source)
XLA Modules:
  0.0 405.1 jit_solution(3510351096055901369)
XLA Ops:
  0.0 0.7 and_select_fusion
  0.7 399.2 %shard_map.37 = f32[8,64,128]{2,1,0:T(8,128)} custom-call(f32[2080,2048]{1,0:T(8,128)} %pressure_ref.1, s32[1,64]{1,0:T(1,128)} %bitcast.25), custom_call_target="tpu_custom_call" | custom-call | tf_op jit(solution)/shard_map/pallas_call | solution.py:277
  399.9 1.2 fusion.11
  401.1 0.2 copy.4
  401.3 0.2 fusion.2
  401.5 1.6 fusion
  403.1 0.7 convolution_bitcast_fusion
  403.8 1.3 copy.5
  (2 shorter events, 0.1 us)
